TPU v7x, 128 devices: a whole 4x4x4 slice. The times are simulated.
128 devices in a mesh: seq: 8 (over x, core), grp: 16 (over z, y).
Axes of the slice: x: 4, y: 4, z: 4, core: 2. Of those that a mesh axis runs over, the one named last changes fastest.
Arguments:
- tokens: bfloat16 [16, 1024, 1536], P('grp', 'seq'), may hold values from -15 to 15
- lengths: int32 [16, 3], P('grp'), may hold values from 1 to 512, 1024 in all within a row
- prompt_adapter: int32 [16, 3], P('grp'), may hold values from 0 to 15
- routes: int32 [16, 1024, 8], P('grp', 'seq'), may hold values from 0 to 39, all different within a row; in each aligned block of 128 rows (0 to 127, 128 to 255, ..., all dimensions but the last counted through in order) at most 40 rows name the same one
- routing_weight: float32 [16, 1024, 8], P('grp', 'seq'), may hold values from 0.1 to 1
- attention_gain: float32 [1536], replicated, may hold values from 0.5 to 1.5
- query_weight: bfloat16 [1536, 1536], replicated, may hold values from -25 to 25
- key_weight: bfloat16 [1536, 512], replicated, may hold values from -0.15625 to 0.15625
- value_weight: bfloat16 [1536, 512], replicated, may hold values from -0.15625 to 0.15625
- output_weight: bfloat16 [1536, 1536], replicated, may hold values from -0.15625 to 0.15625
- adapter_down_maps: bfloat16 [4, 16, 1536, 16], P(None, 'grp'), may hold values from -0.15625 to 0.15625
- adapter_up_query_output: bfloat16 [2, 16, 16, 1536], P(None, 'grp'), may hold values from -1.5 to 1.5
- adapter_up_key_value: bfloat16 [2, 16, 16, 512], P(None, 'grp'), may hold values from -1.5 to 1.5
- expert_gain: float32 [1536], replicated, may hold values from 0.5 to 1.5
- gate_weight: bfloat16 [80, 1536, 256], P('grp'), may hold values from -0.15625 to 0.15625
- up_weight: bfloat16 [80, 1536, 256], P('grp'), may hold values from -0.15625 to 0.15625
- down_weight: bfloat16 [80, 256, 1536], P('grp'), may hold values from -0.25 to 0.25
- closing_gain: float32 [1536], replicated, may hold values from 0.5 to 1.5
- vocab_projection: bfloat16 [1536, 49152], P(None, ('seq', 'grp')), may hold values from -10 to 10
Outputs:
- hidden_out: bfloat16 [16, 1024, 1536], P('grp', 'seq')
- log_probs: float32 [48, 49152], P(None, ('seq', 'grp'))
Inputs may be any that keep to these rules, and one draw needn't show every extreme that they name: The 3 lengths of a group sum to 1024; the longest is exactly 512. `routes`: A token names 8 different experts. Within the 128 tokens of one device no expert is named by more than 40 of them, and in every draw some expert is named by exactly 40 tokens of some device.
All inputs are finite; a program needn't handle non-finite values.
Results may differ from a plain program's by a relative error of at most 0.017.
The roundings to bfloat16 on the way count: a program that leaves them out, or rounds other values in their place, can miss the bound.
Values may be sent and summed in bfloat16 or wider, within the bound.
No kernel may reach another device: no remote copies, remote signals or barrier semaphores. Data moves between devices by JAX's collectives and lax.ppermute only.
A program may use at most 192 MiB of HBM per device.

v0:
```python
import jax
import jax.numpy as jnp
from jax import lax
from jax.sharding import PartitionSpec as P

HEADS = 24
KV_HEADS = 8
HEAD = 64
EXPERTS = 40
TOP = 8
CAP = 40
EPSILON = 1e-05
ROPE_BASE = 10000.0
MASKED = -1e30


def rms_scaled(features, scales):
    features = features.astype(jnp.float32)
    inverse = lax.rsqrt(jnp.mean(features * features, axis=-1, keepdims=True) + EPSILON)
    return (features * inverse * scales).astype(jnp.bfloat16)


def rotate(features, offsets):
    half_size = features.shape[-1] // 2
    frequency = ROPE_BASE ** (-jnp.arange(half_size, dtype=jnp.float32) / half_size)
    angles = offsets.astype(jnp.float32)[:, None, None] * frequency[None, None, :]
    cosine = jnp.cos(angles)
    sines = jnp.sin(angles)
    first_half = features[..., :half_size]
    second = features[..., half_size:]
    return jnp.concatenate(
        [first_half * cosine - second * sines, second * cosine + first_half * sines], axis=-1
    )


def doc_layout(prompt_lens, row_index):
    doc_ends = jnp.cumsum(prompt_lens)
    starts = doc_ends - prompt_lens
    document = jnp.sum((row_index[:, None] >= doc_ends[None, :]).astype(jnp.int32), axis=1)
    member = document[:, None] == jnp.arange(prompt_lens.shape[0], dtype=jnp.int32)[None, :]
    doc_start = jnp.sum(jnp.where(member, starts[None, :], 0), axis=1)
    return (document, row_index - doc_start, member)


def adapter_delta(normalized_rows, selected_experts, down_proj, up_weights):
    low_rank = jnp.einsum(
        "td,adr->tar", normalized_rows, down_proj, preferred_element_type=jnp.float32
    )
    low_rank = (low_rank * selected_experts[:, :, None]).astype(jnp.bfloat16)
    return jnp.einsum("tar,are->te", low_rank, up_weights, preferred_element_type=jnp.float32)


def body(
    tokens,
    lengths,
    prompt_adapter,
    routes,
    routing_weight,
    attention_gain,
    query_weight,
    key_weight,
    value_weight,
    output_weight,
    adapter_down_maps,
    adapter_up_query_output,
    adapter_up_key_value,
    expert_gain,
    gate_weight,
    up_weight,
    down_weight,
    closing_gain,
    vocab_projection,
):
    rows_in = tokens[0]
    tok_count = rows_in.shape[0]
    model_width = rows_in.shape[1]
    prompt_lens = lengths[0]
    owners = prompt_adapter[0]
    ratio = HEADS // KV_HEADS
    logit_scale = HEAD ** (-0.5)
    down_all, wide_all, narrow_all = (
        lax.all_gather(adapter_down_maps, "grp", axis=1, tiled=True),
        lax.all_gather(adapter_up_query_output, "grp", axis=1, tiled=True),
        lax.all_gather(adapter_up_key_value, "grp", axis=1, tiled=True),
    )
    row_index = lax.axis_index("seq") * tok_count + jnp.arange(tok_count, dtype=jnp.int32)
    document, offsets, member = doc_layout(prompt_lens, row_index)
    adapter = jnp.sum(jnp.where(member, owners[None, :], 0), axis=1)
    selected_experts = (
        adapter[:, None] == jnp.arange(down_all.shape[1], dtype=jnp.int32)[None, :]
    ).astype(jnp.float32)
    normalized_rows = rms_scaled(rows_in, attention_gain)
    query_matrix = jnp.dot(
        normalized_rows, query_weight, preferred_element_type=jnp.float32
    ) + adapter_delta(normalized_rows, selected_experts, down_all[0], wide_all[0])
    query_matrix = rotate(query_matrix.reshape(tok_count, HEADS, HEAD), offsets).astype(
        jnp.bfloat16
    )
    query_matrix = query_matrix.reshape(tok_count, KV_HEADS, ratio, HEAD)
    key_matrix = jnp.dot(
        normalized_rows, key_weight, preferred_element_type=jnp.float32
    ) + adapter_delta(normalized_rows, selected_experts, down_all[1], narrow_all[0])
    key_matrix = (
        rotate(key_matrix.reshape(tok_count, KV_HEADS, HEAD), offsets)
        .astype(jnp.bfloat16)
        .reshape(tok_count, KV_HEADS * HEAD)
    )
    value_matrix = (
        jnp.dot(normalized_rows, value_weight, preferred_element_type=jnp.float32)
        + adapter_delta(normalized_rows, selected_experts, down_all[2], narrow_all[1])
    ).astype(jnp.bfloat16)
    running_max = jnp.full((KV_HEADS, ratio, tok_count), MASKED, jnp.float32)
    key_part = lax.all_gather(key_matrix, "seq", axis=0, tiled=True)
    value_part = lax.all_gather(value_matrix, "seq", axis=0, tiled=True)
    key_count = key_part.shape[0]
    key_index = jnp.arange(key_count, dtype=jnp.int32)
    key_doc, _, _ = doc_layout(prompt_lens, key_index)
    allowed = (key_doc[None, :] == document[:, None]) & (key_index[None, :] <= row_index[:, None])
    attention_logits = (
        jnp.einsum(
            "jhlv,phv->hljp",
            query_matrix,
            key_part.reshape(key_count, KV_HEADS, HEAD),
            preferred_element_type=jnp.float32,
        )
        * logit_scale
    )
    attention_logits = jnp.where(allowed[None, None], attention_logits, MASKED)
    new_max = jnp.maximum(running_max, jnp.max(attention_logits, axis=-1))
    weights = jnp.where(allowed[None, None], jnp.exp(attention_logits - new_max[..., None]), 0.0)
    running_sum = jnp.sum(weights, axis=-1)
    weighted_values = jnp.einsum(
        "ukoe,euh->ukoh",
        weights.astype(jnp.bfloat16),
        value_part.reshape(key_count, KV_HEADS, HEAD),
        preferred_element_type=jnp.float32,
    )
    running_max, running_sum, weighted_values = (new_max, running_sum, weighted_values)
    attention_output = (
        (weighted_values / running_sum[..., None])
        .transpose(2, 0, 1, 3)
        .reshape(tok_count, HEADS * HEAD)
        .astype(jnp.bfloat16)
    )
    outside_mask = jnp.dot(
        attention_output, output_weight, preferred_element_type=jnp.float32
    ) + adapter_delta(attention_output, selected_experts, down_all[3], wide_all[1])
    mixed_rows = (rows_in.astype(jnp.float32) + outside_mask).astype(jnp.bfloat16)
    moe_in = rms_scaled(mixed_rows, expert_gain)
    expert_ids = routes[0].reshape(-1)
    flat_weights = routing_weight[0].reshape(-1)
    onehot = (expert_ids[:, None] == jnp.arange(EXPERTS, dtype=jnp.int32)[None, :]).astype(
        jnp.int32
    )
    slot_index = jnp.sum((jnp.cumsum(onehot, axis=0) - onehot) * onehot, axis=1)
    source_row = jnp.arange(expert_ids.shape[0], dtype=jnp.int32) // TOP
    slot_table = (
        jnp.full((EXPERTS * CAP,), tok_count, jnp.int32)
        .at[expert_ids * CAP + slot_index]
        .set(source_row)
        .reshape(EXPERTS, CAP)
    )
    padded = jnp.concatenate([moe_in, jnp.zeros((1, model_width), jnp.bfloat16)], axis=0)
    groups = lax.axis_size("grp")
    slices_here = gate_weight.shape[0]
    outgoing = padded[jnp.repeat(slot_table, 2, axis=0)].reshape(
        groups, slices_here, CAP, model_width
    )
    arrived = lax.all_to_all(outgoing, "grp", split_axis=0, concat_axis=0, tiled=True)
    gate_proj = jnp.einsum(
        "nlcd,ldf->nlcf", arrived, gate_weight, preferred_element_type=jnp.float32
    )
    up_proj = jnp.einsum("nlcd,ldf->nlcf", arrived, up_weight, preferred_element_type=jnp.float32)
    hidden = (jax.nn.silu(gate_proj) * up_proj).astype(jnp.bfloat16)
    halves = jnp.einsum(
        "nlcf,lfd->nlcd", hidden, down_weight, preferred_element_type=jnp.float32
    ).astype(jnp.bfloat16)
    returned = lax.all_to_all(halves, "grp", split_axis=0, concat_axis=0, tiled=True).reshape(
        -1, model_width
    )
    slice_ids = 2 * expert_ids[:, None] + jnp.arange(2, dtype=jnp.int32)[None, :]
    pick_index = slice_ids * CAP + slot_index[:, None]
    picked = returned[pick_index].astype(jnp.float32).reshape(tok_count, TOP * 2, model_width)
    holder = slice_ids // slices_here
    holder_hot = (holder[:, :, None] == jnp.arange(groups, dtype=jnp.int32)[None, None, :]).astype(
        jnp.float32
    )
    holder_hot = (holder_hot * flat_weights[:, None, None]).reshape(tok_count, TOP * 2, groups)
    partial_value = jnp.einsum(
        "tkg,tkd->tgd", holder_hot, picked, precision=lax.Precision.HIGHEST
    ).astype(jnp.bfloat16)
    combined = jnp.sum(partial_value.astype(jnp.float32), axis=1)
    hidden_out = (mixed_rows.astype(jnp.float32) + combined).astype(jnp.bfloat16)
    last_index = jnp.cumsum(prompt_lens) - 1
    selector = (last_index[:, None] == row_index[None, :]).astype(jnp.bfloat16)
    last_rows = jnp.dot(selector, hidden_out, preferred_element_type=jnp.float32)
    last_rows = rms_scaled(last_rows, closing_gain).astype(jnp.float32)
    own_group = (jnp.arange(groups, dtype=jnp.int32) == lax.axis_index("grp")).astype(jnp.float32)
    spread = own_group[:, None, None] * last_rows[None, :, :]
    gathered = lax.psum(spread, ("seq", "grp"))
    final_rows = gathered.reshape(-1, model_width).astype(jnp.bfloat16)
    logits = jnp.dot(final_rows, vocab_projection, preferred_element_type=jnp.float32)
    global_max = lax.pmax(jnp.max(logits, axis=1), ("seq", "grp"))
    global_sum = lax.psum(jnp.sum(jnp.exp(logits - global_max[:, None]), axis=1), ("seq", "grp"))
    log_probs = logits - (global_max + jnp.log(global_sum))[:, None]
    return (hidden_out[None], log_probs)


def solution(mesh):
    placed = (
        P("grp", "seq", None),
        P("grp", None),
        P("grp", None),
        P("grp", "seq", None),
        P("grp", "seq", None),
        P(),
        P(),
        P(),
        P(),
        P(),
        P(None, "grp", None, None),
        P(None, "grp", None, None),
        P(None, "grp", None, None),
        P(),
        P("grp", None, None),
        P("grp", None, None),
        P("grp", None, None),
        P(),
        P(None, ("seq", "grp")),
    )
    return jax.shard_map(
        body,
        mesh=mesh,
        in_specs=placed,
        out_specs=(P("grp", "seq", None), P(None, ("seq", "grp"))),
        check_vma=False,
    )
```

profile of v0, /device:TPU:1, one launch (start us, length us, event | category | flops | bytes accessed | tf_op | source)
XLA Modules:
  0.0 710.5 jit_solution(9158568903717004309)
XLA Ops:
  12.1 22.3 %all_gather.16 = bf16[2,16,16,512]{3,2,1,0:T(8,128)(2,1)S(1)} all-gather(bf16[2,1,16,512]{3,2,1,0:T(8,128)(2,1)} %param.31), channel_id=1, replica_groups=mesh['seq'=8,'grp'=16] {'grp'}, dimensions={1}, use_global_device_ids=true | all-gather | bytes 557056 | tf_op jit(solution)/shard_map/all_gather | solution.py:84
  34.4 11.3 %reduce-window.11 = s32[40,8,128]{2,1,0:T(8,128)S(1)} reduce-window(s32[40,8,128]{2,1,0:T(8,128)S(1)} %fusion.60, s32[]{:T(128)} %constant.32.clone.1), window={size=1x1x128 pad=0_0x0_0x127_0}, to_apply=%region_9.10 | reduce-window | flops 5201920 | bytes 327684 | tf_op jit(solution)/shard_map/reduce-window.1
  46.4 4.3 scatter_custom_fusion
  53.3 8.4 %all-gather.5.cloned.1.call-done = bf16[4,16,1536,16]{2,3,1,0:T(8,128)(2,1)} async-done(((bf16[4,1,1536,16]{2,3,1,0:T(8,128)(2,1)}), bf16[4,16,1536,16]{2,3,1,0:T(8,128)(2,1)}) %all-gather.5.cloned.1.call-update) | async-done | bytes 3145744 | tf_op jit(solution)/shard_map/all_gather | solution.py:82
  61.7 3.2 fusion.93
  70.3 35.7 %all-gather.9.cloned.1.call-done = bf16[2,16,16,1536]{3,2,1,0:T(8,128)(2,1)} async-done(((bf16[2,1,16,1536]{3,2,1,0:T(8,128)(2,1)}), bf16[2,16,16,1536]{3,2,1,0:T(8,128)(2,1)}) %all-gather.9.cloned.1.call-update) | async-done | bytes 1572880 | tf_op jit(solution)/shard_map/all_gather | solution.py:83
  115.3 16.3 %all-gather.7.cloned.1.call-done = bf16[1024,512]{0,1:T(8,128)(2,1)} async-done(((bf16[128,512]{0,1:T(8,128)(2,1)}), bf16[1024,512]{0,1:T(8,128)(2,1)}) %all-gather.7.cloned.1.call-update) | async-done | bytes 1048592 | tf_op jit(solution)/shard_map/all_gather | solution.py:113
  134.8 4.5 copy-done.2
  142.4 15.8 %all-gather.11.cloned.1.call-done = bf16[1024,512]{1,0:T(8,128)(2,1)} async-done(((bf16[128,512]{1,0:T(8,128)(2,1)}), bf16[1024,512]{1,0:T(8,128)(2,1)}) %all-gather.11.cloned.1.call-update) | async-done | bytes 1048592 | tf_op jit(solution)/shard_map/all_gather | solution.py:114
  160.5 8.1 %fusion.40 = bf16[128,8,3,64]{0,3,2,1:T(8,128)(2,1)S(1)} fusion(bf16[1024,8,64,1]{0,2,3,1:T(8,128)(2,1)} %bitcast.215, f32[8,1024,128,3]{2,1,3,0:T(8,128)} %copy-done.2, f32[8,3,128]{2,1,0:T(4,128)S(1)} %broadcast_maximum_fusion, pred[128,1024]{0,1:T(8,128)(4,1)S(1)} %fusion.51, f32[128,8,3]{0,2,1:T(4,128)S(1)} %bitcast.233), kind=kOutput, calls=%fused_computation.49 | convolution fusion | flops 418775040 | bytes 14180352 | tf_op jit(solution)/shard_map/ukoe,euh->ukoh/dot_general | solution.py:132
  169.2 3.3 multiply_reduce_fusion
  172.7 11.9 %gather_fusion = bf16[3200,1536]{1,0:T(8,128)(2,1)} fusion(bf16[129,1536]{1,0:T(8,128)(2,1)S(1)} %concatenate.20, s32[4096]{0:T(1024)S(1)} %pad_clamp_fusion), kind=kCustom, calls=%fused_computation | custom fusion | bytes 19673600 | tf_op jit(solution)/shard_map/gather | solution.py:166
  184.5 117.5 %all_to_all.10 = bf16[16,5,40,1536]{3,2,1,0:T(8,128)(2,1)S(1)} all-to-all(bf16[16,5,40,1536]{3,2,1,0:T(8,128)(2,1)} %bitcast.208), channel_id=1, replica_groups=mesh['seq'=8,'grp'=16] {'grp'}, dimensions={0} | all-to-all | bytes 19660800 | tf_op jit(solution)/shard_map/all_to_all | solution.py:169
  302.1 3.8 copy-done.3
  305.8 4.6 fusion.6
  310.5 13.4 %fusion.1 = bf16[16,5,40,1536]{3,2,0,1:T(8,128)(2,1)} fusion(bf16[5,256,1536]{2,1,0:T(8,128)(2,1)} %param.35, f32[5,16,40,256]{3,2,1,0:T(8,128)} %fusion.6, bf16[5,1536,256]{2,1,0:T(8,128)(2,1)} %param.34, bf16[16,5,40,1536]{3,2,1,0:T(8,128)(2,1)} %copy-done.3), kind=kOutput, calls=%fused_computation.8 | convolution fusion | flops 5042995200 | bytes 30801920 | tf_op jit(solution)/shard_map/nlcf,lfd->nlcd/dot_general | solution.py:175
  323.9 8.3 %copy.70 = bf16[16,5,40,1536]{3,2,1,0:T(8,128)(2,1)} copy(bf16[16,5,40,1536]{3,2,0,1:T(8,128)(2,1)} %fusion.1) | data formatting | bytes 19660800 | tf_op jit(solution)/shard_map/convert_element_type | solution.py:177
  332.2 4.9 all-to-all-start.1
  338.2 141.3 %all-to-all-done.1 = bf16[16,5,40,1536]{3,2,1,0:T(8,128)(2,1)} async-done(((bf16[16,5,40,1536]{3,2,1,0:T(8,128)(2,1)}), bf16[16,5,40,1536]{3,2,1,0:T(8,128)(2,1)}, u32[]{:S(2)}, u32[]{:S(2)}) %all-to-all-start.1) | async-done | bytes 9830432 | tf_op jit(solution)/shard_map/all_to_all | solution.py:178
  479.5 18.3 %gather_fusion.1 = bf16[2048,1536]{1,0:T(8,128)(2,1)} fusion(bf16[3200,1536]{1,0:T(8,128)(2,1)} %bitcast.65, s32[2048]{0:T(1024)S(1)} %broadcast_clamp_fusion), kind=kCustom, calls=%fused_computation.1 | custom fusion | bytes 12591104 | tf_op jit(solution)/shard_map/gather | solution.py:183
  497.8 9.2 %convert_reduce_fusion = f32[128,1536]{1,0:T(8,128)S(1)} fusion(bf16[128,16,1536]{2,1,0:T(8,128)(2,1)} %bitcast.209, f32[128,16]{1,0:T(8,128)S(1)} %copy.62, s32[128,16]{1,0:T(8,128)S(1)} %copy.61), kind=kOutput, calls=%fused_computation.4 | convolution fusion | flops 613285888 | bytes 7094272 | tf_op jit(solution)/shard_map/tkg,tkd->tgd/dot_general | solution.py:189
  507.6 66.9 %all-reduce.2 = bf16[16,3,1536]{2,1,0:T(4,128)(2,1)S(1)} all-reduce(f32[16,3,1536]{2,1,0:T(4,128)S(1)} %broadcast_multiply_fusion), channel_id=1, replica_groups=mesh['seq'=8,'grp'=16] {'seq','grp'}, use_global_device_ids=true, to_apply=%region_15.16 | all-reduce | flops 73728 | bytes 442368 | tf_op jit(solution)/shard_map/psum | solution.py:200
  576.4 64.0 %pmax.7 = f32[48]{0:T(128)S(1)} all-reduce(f32[48]{0:T(128)S(1)} %get-tuple-element.22), channel_id=1, replica_groups=mesh['seq'=8,'grp'=16] {'seq','grp'}, use_global_device_ids=true, to_apply=%region_17.18 | all-reduce | flops 48 | bytes 384 | tf_op jit(solution)/shard_map/pmax | solution.py:203
  640.6 62.6 %psum.15 = f32[48]{0:T(128)S(1)} all-reduce(f32[48]{0:T(128)S(1)} %exponential_reduce_fusion), channel_id=1, replica_groups=mesh['seq'=8,'grp'=16] {'seq','grp'}, use_global_device_ids=true, to_apply=%region_19.20 | all-reduce | flops 48 | bytes 384 | tf_op jit(solution)/shard_map/psum | solution.py:204
  (110 shorter events, 36.2 us)
Async XLA Ops:
  7.2 58.4 %copy-start = (bf16[1536,512]{1,0:T(8,128)(2,1)S(1)}, bf16[1536,512]{1,0:T(8,128)(2,1)}, u32[]{:S(2)}) copy-start(bf16[1536,512]{1,0:T(8,128)(2,1)} %param.26) | copy-start | bytes 4718596
  7.2 57.7 %copy-start.4 = (bf16[1,128,1536]{2,1,0:T(8,128)(2,1)S(1)}, bf16[1,128,1536]{2,1,0:T(8,128)(2,1)}, u32[]{:S(2)}) copy-start(bf16[1,128,1536]{2,1,0:T(8,128)(2,1)} %param.19) | copy-start | bytes 1179652
  7.2 57.7 %copy-start.7 = (f32[1536]{0:T(1024)S(1)}, f32[1536]{0:T(1024)}, u32[]{:S(2)}) copy-start(f32[1536]{0:T(1024)} %param.24) | copy-start | bytes 18436
  7.2 54.5 %all-gather.5.cloned.1.call-start = ((), (), s32[]{:S(2)}) async-start(), calls=%async_computation.2 | async-start | bytes 3342336 | tf_op jit(solution)/shard_map/all_gather | solution.py:82
  7.9 98.1 %all-gather.9.cloned.1.call-start = ((), (), s32[]{:S(2)}) async-start(), calls=%async_computation.4 | async-start | bytes 1671168 | tf_op jit(solution)/shard_map/all_gather | solution.py:83
  8.7 122.9 %all-gather.7.cloned.1.call-start = ((), (), s32[]{:S(2)}) async-start(), calls=%async_computation.3 | async-start | bytes 1179648 | tf_op jit(solution)/shard_map/all_gather | solution.py:113
  68.5 89.7 %all-gather.11.cloned.1.call-start = ((), (), s32[]{:S(2)}) async-start(), calls=%async_computation.5 | async-start | bytes 1179648 | tf_op jit(solution)/shard_map/all_gather | solution.py:114
  134.8 4.6 copy-start.2
  160.5 8.4 %copy-start.5 = (bf16[2,16,16,1536]{3,2,1,0:T(8,128)(2,1)S(1)}, bf16[2,16,16,1536]{3,2,1,0:T(8,128)(2,1)}, u32[]{:S(2)}) copy-start(bf16[2,16,16,1536]{3,2,1,0:T(8,128)(2,1)} %all-gather.9.cloned.1.call-done) | copy-start | bytes 4718596
  168.5 4.0 copy-start.8
  184.5 121.3 %copy-start.11 = (bf16[5,1536,256]{2,1,0:T(8,128)(2,1)S(1)}, bf16[5,1536,256]{2,1,0:T(8,128)(2,1)}, u32[]{:S(2)}) copy-start(bf16[5,1536,256]{2,1,0:T(8,128)(2,1)} %param.33) | copy-start | bytes 11796484
  302.1 3.8 copy-start.3
  332.2 5.8 copy-start.10
  332.2 147.3 %all-to-all-start.1 = ((bf16[16,5,40,1536]{3,2,1,0:T(8,128)(2,1)}), bf16[16,5,40,1536]{3,2,1,0:T(8,128)(2,1)}, u32[]{:S(2)}, u32[]{:S(2)}) async-start(bf16[16,5,40,1536]{3,2,1,0:T(8,128)(2,1)} %copy.70), calls=%async_computation.1 | async-start | bytes 19660800 | tf_op jit(solution)/shard_map/all_to_all | solution.py:178
  497.8 206.1 %copy-start.1 = (bf16[1536,512]{1,0:T(8,128)(2,1)S(1)}, bf16[1536,512]{1,0:T(8,128)(2,1)}, u32[]{:S(2)}) copy-start(bf16[1536,512]{1,0:T(8,128)(2,1)} %param.26) | copy-start | bytes 4718596
  497.8 9.6 %copy-start.9 = (f32[1536]{0:T(1024)S(1)}, f32[1536]{0:T(1024)}, u32[]{:S(2)}) copy-start(f32[1536]{0:T(1024)} %param.36) | copy-start | bytes 18436
  507.1 196.8 %copy-start.6 = (bf16[128,1536]{1,0:T(8,128)(2,1)}, bf16[128,1536]{1,0:T(8,128)(2,1)S(1)}, u32[]{:S(2)}) copy-start(bf16[128,1536]{1,0:T(8,128)(2,1)S(1)} %add_convert_fusion) | copy-start | bytes 1179652
Sparse Core Ops, SparseCore 0:
  10.2 51.4 all-gather.4
  63.8 42.1 all-gather.8
  107.7 23.8 all-gather.6
  133.8 24.3 all-gather.10
where the time goes:
time: 712 us; the launch traced here: 710 us
  blocking collectives  333 us (47%)
  waiting for transfers between devices  219 us (31%)
  local copies, waits for them, and re-layouts  60.3 us (8%)
  matrix products  56.6 us (8%)
  other arithmetic  21.7 us (3%)
  between operations  14.3 us (2%)
    all_to_all x1, waiting for transfers between devices, body(): lax.all_to_all(halves, 'grp', split_axis=0, concat_axis=0, tiled=True)  141 us
    all_to_all x1, blocking collectives, body(): lax.all_to_all(outgoing, 'grp', split_axis=0, concat_axis=0, tiled=True)  118 us
    psum x1, blocking collectives, body(): gathered = lax.psum(spread, ('seq', 'grp'))  66.9 us
    pmax x1, blocking collectives, body(): global_max = lax.pmax(jnp.max(logits, axis=1), ('seq', 'grp'))  64 us
    psum x1, blocking collectives, body(): lax.psum(jnp.sum(jnp.exp(logits - global_max[:, None]), axis=1), ('seq',...  62.6 us
    all_gather x1, waiting for transfers between devices, body(): lax.all_gather(adapter_up_query_output, 'grp', axis=1, tiled=True)  35.7 us
    all_gather x1, blocking collectives, body(): lax.all_gather(adapter_up_key_value, 'grp', axis=1, tiled=True)  22.3 us
    gather x1, local copies, waits for them, and re-layouts, body(): returned[pick_index].astype(jnp.float32)  18.3 us
  transfers between devices with their start and end apart: 5, of which 5 were waited for; matrix products, arithmetic and copies ran while one was open for 7% of the time, Pallas kernels for 0%

commit v1 on v0

--- a/solution.py
+++ b/solution.py
@@ -12,6 +12,13 @@
 EPSILON = 1e-05
 ROPE_BASE = 10000.0
 MASKED = -1e30
+
+
+def exchange_gather(shard, axis, dim):
+    size = lax.axis_size(axis)
+    parts = jnp.stack([shard for _ in range(size)])
+    parts = lax.all_to_all(parts, axis, split_axis=0, concat_axis=0)
+    return jnp.concatenate(parts, axis=dim)
 
 
 def rms_scaled(features, scales):
@@ -111,7 +118,7 @@
     ).astype(jnp.bfloat16)
     running_max = jnp.full((KV_HEADS, ratio, tok_count), MASKED, jnp.float32)
     key_part = lax.all_gather(key_matrix, "seq", axis=0, tiled=True)
-    value_part = lax.all_gather(value_matrix, "seq", axis=0, tiled=True)
+    value_part = exchange_gather(value_matrix, "seq", 0)
     key_count = key_part.shape[0]
     key_index = jnp.arange(key_count, dtype=jnp.int32)
     key_doc, _, _ = doc_layout(prompt_lens, key_index)

time: 712 us -> 683 us (0.959)
  waiting for transfers between devices: 219 us -> 193 us
  matrix products: 56.6 us -> 47.8 us
    all_gather x1 -> x0, waiting for transfers between devices: 15.8 us -> none  [body(): value_part = lax.all_gather(value_matrix, 'seq', axis=0, tiled=True)]
    all_gather x1, waiting for transfers between devices: 35.7 us -> 26.2 us  [body(): lax.all_gather(adapter_up_query_output, 'grp', axis=1, tiled=True)]
  transfers between devices with their start and end apart: 5 -> 5, of which waited for: 5 -> 4; matrix products, arithmetic and copies ran while one was open for 7% -> 7% of each run, Pallas kernels for 0% -> 0%
where the time goes in v1:
time: 683 us; the launch traced here: 682 us
  blocking collectives  334 us (49%)
  waiting for transfers between devices  193 us (28%)
  local copies, waits for them, and re-layouts  57.1 us (8%)
  matrix products  47.8 us (7%)
  other arithmetic  25.1 us (4%)
  between operations  14.4 us (2%)
  starting transfers between devices  10.6 us (2%)
    all_to_all x1, waiting for transfers between devices, body(): lax.all_to_all(halves, 'grp', split_axis=0, concat_axis=0, tiled=True)  141 us
    all_to_all x1, blocking collectives, body(): lax.all_to_all(outgoing, 'grp', split_axis=0, concat_axis=0, tiled=True)  118 us
    psum x1, blocking collectives, body(): gathered = lax.psum(spread, ('seq', 'grp'))  68.2 us
    psum x1, blocking collectives, body(): lax.psum(jnp.sum(jnp.exp(logits - global_max[:, None]), axis=1), ('seq',...  64 us
    pmax x1, blocking collectives, body(): global_max = lax.pmax(jnp.max(logits, axis=1), ('seq', 'grp'))  62.5 us
    all_gather x1, waiting for transfers between devices, body(): lax.all_gather(adapter_up_query_output, 'grp', axis=1, tiled=True)  26.2 us
    all_gather x1, blocking collectives, body(): lax.all_gather(adapter_up_key_value, 'grp', axis=1, tiled=True)  22.2 us
    all_gather x1, waiting for transfers between devices, body(): key_part = lax.all_gather(key_matrix, 'seq', axis=0, tiled=True)  18.6 us
  transfers between devices with their start and end apart: 5, of which 4 were waited for; matrix products, arithmetic and copies ran while one was open for 7% of the time, Pallas kernels for 0%

profile of v1, /device:TPU:1, one launch (start us, length us, event | category | flops | bytes accessed | tf_op | source)
XLA Modules:
  0.0 682.3 jit_solution(6585196381711706534)
XLA Ops:
  12.7 22.2 %all_gather.13 = bf16[2,16,16,512]{3,2,1,0:T(8,128)(2,1)S(1)} all-gather(bf16[2,1,16,512]{3,2,1,0:T(8,128)(2,1)} %param.31), channel_id=1, replica_groups=mesh['seq'=8,'grp'=16] {'grp'}, dimensions={1}, use_global_device_ids=true | all-gather | bytes 557056 | tf_op jit(solution)/shard_map/all_gather | solution.py:91
  34.9 11.3 %reduce-window.11 = s32[40,8,128]{2,1,0:T(8,128)S(1)} reduce-window(s32[40,8,128]{2,1,0:T(8,128)S(1)} %fusion.65, s32[]{:T(128)} %constant.32.clone.1), window={size=1x1x128 pad=0_0x0_0x127_0}, to_apply=%region_9.10 | reduce-window | flops 5201920 | bytes 327684 | tf_op jit(solution)/shard_map/reduce-window.1
  47.5 4.3 scatter_custom_fusion
  56.2 5.6 all-gather.4.cloned.1.call-done
  61.8 3.2 fusion.98
  74.0 5.4 all-to-all-start
  79.9 26.2 %all-gather.8.cloned.1.call-done = bf16[2,16,16,1536]{3,2,1,0:T(8,128)(2,1)} async-done(((bf16[2,1,16,1536]{3,2,1,0:T(8,128)(2,1)}), bf16[2,16,16,1536]{3,2,1,0:T(8,128)(2,1)}) %all-gather.8.cloned.1.call-update) | async-done | bytes 1572880 | tf_op jit(solution)/shard_map/all_gather | solution.py:90
  107.6 3.2 convolution_add_fusion.1
  113.2 18.6 %all-gather.6.cloned.1.call-done = bf16[1024,512]{0,1:T(8,128)(2,1)} async-done(((bf16[128,512]{0,1:T(8,128)(2,1)}), bf16[1024,512]{0,1:T(8,128)(2,1)}) %all-gather.6.cloned.1.call-update) | async-done | bytes 1048592 | tf_op jit(solution)/shard_map/all_gather | solution.py:120
  131.8 3.1 fusion
  138.0 3.5 fusion.43
  143.4 11.9 %gather_fusion = bf16[3200,1536]{1,0:T(8,128)(2,1)} fusion(bf16[129,1536]{1,0:T(8,128)(2,1)S(1)} %concatenate.20, s32[4096]{0:T(1024)S(1)} %pad_clamp_fusion), kind=kCustom, calls=%fused_computation | custom fusion | bytes 19673600 | tf_op jit(solution)/shard_map/gather | solution.py:173
  155.2 117.5 %all_to_all.15 = bf16[16,5,40,1536]{3,2,1,0:T(8,128)(2,1)S(1)} all-to-all(bf16[16,5,40,1536]{3,2,1,0:T(8,128)(2,1)} %bitcast.211), channel_id=1, replica_groups=mesh['seq'=8,'grp'=16] {'grp'}, dimensions={0} | all-to-all | bytes 19660800 | tf_op jit(solution)/shard_map/all_to_all | solution.py:176
  272.8 3.8 copy-done.2
  276.6 4.6 fusion.6
  281.2 13.4 %fusion.1 = bf16[16,5,40,1536]{3,2,0,1:T(8,128)(2,1)} fusion(bf16[5,256,1536]{2,1,0:T(8,128)(2,1)} %param.35, f32[5,16,40,256]{3,2,1,0:T(8,128)} %fusion.6, bf16[5,1536,256]{2,1,0:T(8,128)(2,1)} %param.34, bf16[16,5,40,1536]{3,2,1,0:T(8,128)(2,1)} %copy-done.2), kind=kOutput, calls=%fused_computation.8 | convolution fusion | flops 5042995200 | bytes 30801920 | tf_op jit(solution)/shard_map/nlcf,lfd->nlcd/dot_general | solution.py:182
  294.6 8.3 %copy.72 = bf16[16,5,40,1536]{3,2,1,0:T(8,128)(2,1)} copy(bf16[16,5,40,1536]{3,2,0,1:T(8,128)(2,1)} %fusion.1) | data formatting | bytes 19660800 | tf_op jit(solution)/shard_map/convert_element_type | solution.py:184
  302.9 5.1 all-to-all-start.2
  309.1 141.1 %all-to-all-done.2 = bf16[16,5,40,1536]{3,2,1,0:T(8,128)(2,1)} async-done(((bf16[16,5,40,1536]{3,2,1,0:T(8,128)(2,1)}), bf16[16,5,40,1536]{3,2,1,0:T(8,128)(2,1)}, u32[]{:S(2)}, u32[]{:S(2)}) %all-to-all-start.2) | async-done | bytes 9830432 | tf_op jit(solution)/shard_map/all_to_all | solution.py:185
  450.1 18.3 %gather_fusion.1 = bf16[2048,1536]{1,0:T(8,128)(2,1)} fusion(bf16[3200,1536]{1,0:T(8,128)(2,1)} %bitcast.63, s32[2048]{0:T(1024)S(1)} %broadcast_clamp_fusion), kind=kCustom, calls=%fused_computation.1 | custom fusion | bytes 12591104 | tf_op jit(solution)/shard_map/gather | solution.py:190
  468.5 9.2 %convert_reduce_fusion = f32[128,1536]{1,0:T(8,128)S(1)} fusion(bf16[128,16,1536]{2,1,0:T(8,128)(2,1)} %bitcast.212, f32[128,16]{1,0:T(8,128)S(1)} %copy.64, s32[128,16]{1,0:T(8,128)S(1)} %copy.63), kind=kOutput, calls=%fused_computation.4 | convolution fusion | flops 613285888 | bytes 7094272 | tf_op jit(solution)/shard_map/tkg,tkd->tgd/dot_general | solution.py:196
  478.3 68.2 %all-reduce.2 = bf16[16,3,1536]{2,1,0:T(4,128)(2,1)S(1)} all-reduce(f32[16,3,1536]{2,1,0:T(4,128)S(1)} %broadcast_multiply_fusion), channel_id=1, replica_groups=mesh['seq'=8,'grp'=16] {'seq','grp'}, use_global_device_ids=true, to_apply=%region_15.16 | all-reduce | flops 73728 | bytes 442368 | tf_op jit(solution)/shard_map/psum | solution.py:207
  548.3 62.5 %pmax.7 = f32[48]{0:T(128)S(1)} all-reduce(f32[48]{0:T(128)S(1)} %get-tuple-element.22), channel_id=1, replica_groups=mesh['seq'=8,'grp'=16] {'seq','grp'}, use_global_device_ids=true, to_apply=%region_17.18 | all-reduce | flops 48 | bytes 384 | tf_op jit(solution)/shard_map/pmax | solution.py:210
  611.1 64.0 %psum.15 = f32[48]{0:T(128)S(1)} all-reduce(f32[48]{0:T(128)S(1)} %exponential_reduce_fusion), channel_id=1, replica_groups=mesh['seq'=8,'grp'=16] {'seq','grp'}, use_global_device_ids=true, to_apply=%region_19.20 | all-reduce | flops 48 | bytes 384 | tf_op jit(solution)/shard_map/psum | solution.py:211
  (147 shorter events, 33.4 us)
Async XLA Ops:
  7.2 58.5 %copy-start = (bf16[1536,512]{1,0:T(8,128)(2,1)S(1)}, bf16[1536,512]{1,0:T(8,128)(2,1)}, u32[]{:S(2)}) copy-start(bf16[1536,512]{1,0:T(8,128)(2,1)} %param.26) | copy-start | bytes 4718596
  7.2 57.8 %copy-start.3 = (bf16[1,128,1536]{2,1,0:T(8,128)(2,1)S(1)}, bf16[1,128,1536]{2,1,0:T(8,128)(2,1)}, u32[]{:S(2)}) copy-start(bf16[1,128,1536]{2,1,0:T(8,128)(2,1)} %param.19) | copy-start | bytes 1179652
  7.2 57.8 %copy-start.11 = (f32[1536]{0:T(1024)S(1)}, f32[1536]{0:T(1024)}, u32[]{:S(2)}) copy-start(f32[1536]{0:T(1024)} %param.24) | copy-start | bytes 18436
  7.2 54.6 %all-gather.4.cloned.1.call-start = ((), (), s32[]{:S(2)}) async-start(), calls=%async_computation.3 | async-start | bytes 3342336 | tf_op jit(solution)/shard_map/all_gather | solution.py:89
  7.9 98.2 %all-gather.8.cloned.1.call-start = ((), (), s32[]{:S(2)}) async-start(), calls=%async_computation.5 | async-start | bytes 1671168 | tf_op jit(solution)/shard_map/all_gather | solution.py:90
  8.7 123.1 %all-gather.6.cloned.1.call-start = ((), (), s32[]{:S(2)}) async-start(), calls=%async_computation.4 | async-start | bytes 1179648 | tf_op jit(solution)/shard_map/all_gather | solution.py:120
  9.7 46.5 %copy-start.14 = (s32[1024]{0:T(1024)}, s32[1024]{0:T(1024)S(1)}, u32[]{:S(2)}) copy-start(s32[1024]{0:T(1024)S(1)} %broadcast_in_dim_reshape_squeeze.2) | copy-start | bytes 12292
  11.0 45.2 %copy-start.22 = (s32[128]{0:T(128)}, s32[128]{0:T(128)S(1)}, u32[]{:S(2)}) copy-start(s32[128]{0:T(128)S(1)} %iota_add_fusion) | copy-start | bytes 1540
  11.8 34.6 %copy-start.24 = (s32[3,1]{0,1:T(1,128)}, s32[3,1]{0,1:T(1,128)S(1)}, u32[]{:S(2)}) copy-start(s32[3,1]{0,1:T(1,128)S(1)} %reduce-window.10) | copy-start | bytes 40
  54.6 10.9 %copy-start.19 = (f32[128]{0:T(128)}, f32[128]{0:T(128)S(1)}, u32[]{:S(2)}) copy-start(f32[128]{0:T(128)S(1)} %add_rsqrt_fusion.2) | copy-start | bytes 1540
  66.8 12.7 %copy-start.20 = (f32[128]{0:T(128)S(1)}, f32[128]{0:T(128)}, u32[]{:S(2)}) copy-start(f32[128]{0:T(128)} %copy-done.19) | copy-start | bytes 1540
  74.0 37.0 %copy-start.9 = (f32[128,32]{0,1:T(8,128)S(1)}, f32[128,32]{0,1:T(8,128)}, u32[]{:S(2)}) copy-start(f32[128,32]{0,1:T(8,128)} %get-tuple-element.14) | copy-start | bytes 49156
  74.0 37.0 %copy-start.10 = (f32[128,32]{0,1:T(8,128)S(1)}, f32[128,32]{0,1:T(8,128)}, u32[]{:S(2)}) copy-start(f32[128,32]{0,1:T(8,128)} %get-tuple-element.15) | copy-start | bytes 49156
  74.0 37.1 %all-to-all-start = ((bf16[8,128,512]{1,2,0:T(8,128)(2,1)}), bf16[8,128,512]{1,2,0:T(8,128)(2,1)S(1)}, u32[]{:S(2)}, u32[]{:S(2)}) async-start(bf16[8,128,512]{1,2,0:T(8,128)(2,1)} %stack.2), calls=%async_computation | async-start | bytes 2097152 | tf_op jit(solution)/shard_map/all_to_all | solution.py:20
  107.6 24.2 %copy-start.7 = (pred[128,1024]{0,1:T(8,128)(4,1)S(1)}, pred[128,1024]{0,1:T(8,128)(4,1)}, u32[]{:S(2)}) copy-start(pred[128,1024]{0,1:T(8,128)(4,1)} %fusion.56) | copy-start | bytes 393220
  134.9 7.3 %slice-start = ((s8[4718592]{0:T(1024)(128)(4,1)}), s8[4194304]{0:T(1024)(128)(4,1)S(1)}, s32[]{:S(2)}) async-start(s8[4718592]{0:T(1024)(128)(4,1)} %bitcast.213), calls=%async_computation.6 | async-start | bytes 8388608
  155.2 121.3 %copy-start.26 = (bf16[5,1536,256]{2,1,0:T(8,128)(2,1)S(1)}, bf16[5,1536,256]{2,1,0:T(8,128)(2,1)}, u32[]{:S(2)}) copy-start(bf16[5,1536,256]{2,1,0:T(8,128)(2,1)} %param.33) | copy-start | bytes 11796484
  302.9 6.0 copy-start.21
  302.9 6.1 copy-start.25
  302.9 147.2 %all-to-all-start.2 = ((bf16[16,5,40,1536]{3,2,1,0:T(8,128)(2,1)}), bf16[16,5,40,1536]{3,2,1,0:T(8,128)(2,1)}, u32[]{:S(2)}, u32[]{:S(2)}) async-start(bf16[16,5,40,1536]{3,2,1,0:T(8,128)(2,1)} %copy.72), calls=%async_computation.2 | async-start | bytes 19660800 | tf_op jit(solution)/shard_map/all_to_all | solution.py:185
  468.5 207.3 %copy-start.1 = (bf16[1536,512]{1,0:T(8,128)(2,1)S(1)}, bf16[1536,512]{1,0:T(8,128)(2,1)}, u32[]{:S(2)}) copy-start(bf16[1536,512]{1,0:T(8,128)(2,1)} %param.26) | copy-start | bytes 4718596
  468.5 9.3 %copy-start.23 = (s32[128]{0:T(128)S(1)}, s32[128]{0:T(128)}, u32[]{:S(2)}) copy-start(s32[128]{0:T(128)} %copy-done.22) | copy-start | bytes 1540
  468.5 9.6 %copy-start.18 = (f32[1536]{0:T(1024)S(1)}, f32[1536]{0:T(1024)}, u32[]{:S(2)}) copy-start(f32[1536]{0:T(1024)} %param.36) | copy-start | bytes 18436
  477.8 198.0 %copy-start.6 = (bf16[128,1536]{1,0:T(8,128)(2,1)}, bf16[128,1536]{1,0:T(8,128)(2,1)S(1)}, u32[]{:S(2)}) copy-start(bf16[128,1536]{1,0:T(8,128)(2,1)S(1)} %add_convert_fusion) | copy-start | bytes 1179652
  (10 other events, 36.8 us)
Sparse Core Ops, SparseCore 0:
  10.2 51.5 all-gather.3
  63.9 42.1 all-gather.7
  107.8 23.8 all-gather.5
